TPU v7x, 256 devices: a whole 4x4x8 slice. The times are simulated.
256 devices in a mesh: seq: 32 (over z_hi, y, core), fsdp: 8 (over z_lo, x).
Axes of the slice: x: 4, y: 4, z: 8 (z_hi: 4, z_lo: 2; z = z_hi * 2 + z_lo), core: 2. Of those that a mesh axis runs over, the one named last changes fastest.
Arguments:
- tokens: bfloat16 [32768, 1280], P('seq'), may hold values from -64 to 64
- cotangent: bfloat16 [32768, 1280], P('seq'), may hold values from -6 to 6
- raster_dest: int32 [32768], P('seq'), may hold values from 0 to 32767, as said below
- keep_mask: int32 [512, 16, 4096], P('seq', 'fsdp'), may hold values 0 or 1
- qkv_weight: bfloat16 [1280, 3840], P('seq', 'fsdp'), may hold values from -0.15625 to 0.15625
- out_weight: bfloat16 [1280, 1280], P('seq', 'fsdp'), may hold values from -0.15625 to 0.15625
Outputs:
- attended: bfloat16 [32768, 1280], P('seq', 'fsdp')
- grad_tokens: bfloat16 [32768, 1280], P('seq', 'fsdp')
- grad_qkv: float32 [1280, 3840], P('seq', 'fsdp')
- grad_out: float32 [1280, 1280], P('seq', 'fsdp')
Inputs may be any that keep to these rules, and one draw needn't show every extreme that they name: `raster_dest`: A permutation. Raster rows form bands of 2048 rows (8 patch rows of 256 patches); band b holds 32 windows of 8 by 8 patches, which go one to each block of 1024 window-order rows, in an order drawn for each band; inside its block, band b's window takes rows b * 64 to (b + 1) * 64 - 1, its patches in raster order.
All inputs are finite; a program needn't handle non-finite values. No bound on the sum of `keep_mask` on one device may be relied on, other than what follows from the above.
Results may differ from a plain program's by a relative error of at most 0.025.
The roundings to bfloat16 on the way count: a program that leaves them out, or rounds other values in their place, can miss the bound.
Values may be sent and summed in bfloat16 or wider, within the bound.
No kernel may reach another device: no remote copies, remote signals or barrier semaphores. Data moves between devices by JAX's collectives and lax.ppermute only.
A program may use at most 64 MiB of HBM per device.

v0:
```python
import jax
import jax.numpy as jnp
from jax import lax
from jax.sharding import PartitionSpec as P

HEAD_DIM = 80
WIN = 8
WIN_TOK = 64
INV_KEEP = 1.0 / 0.9


def to_half(values):
    return lax.optimization_barrier(values.astype(jnp.bfloat16))


def head_total(partial_value):
    rounded = to_half(partial_value).astype(jnp.float32)
    return lax.psum_scatter(
        rounded.astype(jnp.bfloat16), "fsdp", scatter_dimension=1, tiled=True
    ).astype(jnp.float32)


def per_device(tokens, cotangent, raster_dest, keep_mask, qkv_weight, out_weight):
    seq_count = lax.axis_size("seq")
    tok_dev = tokens.shape[0]
    score_scale = HEAD_DIM ** (-0.5)
    windows_local = tok_dev // WIN_TOK
    heads_local = keep_mask.shape[1]
    send_order = jnp.argsort(raster_dest)
    back_order = jnp.argsort(send_order)
    slot_index = jnp.arange(tok_dev, dtype=jnp.int32)
    band_index = slot_index // WIN_TOK
    patch_row = slot_index % WIN_TOK // WIN
    source = (band_index * WIN_TOK * seq_count + patch_row * WIN * seq_count) // tok_dev
    recv_slot = jnp.argsort(source * tok_dev + slot_index)
    slot_recv = jnp.argsort(recv_slot)

    def restore(window_rows):
        outgoing = window_rows[recv_slot]
        returned = lax.all_to_all(outgoing, "seq", split_axis=0, concat_axis=0, tiled=True)
        return returned[back_order]

    qkv_full, out_full = (
        lax.all_gather(qkv_weight, "seq", axis=0, tiled=True),
        lax.all_gather(out_weight, "seq", axis=0, tiled=True),
    )
    windowed = lax.all_to_all(tokens[send_order], "seq", split_axis=0, concat_axis=0, tiled=True)[
        slot_recv
    ]
    cot_window = lax.all_to_all(
        cotangent[send_order], "seq", split_axis=0, concat_axis=0, tiled=True
    )[slot_recv]
    projected = jnp.dot(windowed, qkv_full, preferred_element_type=jnp.float32).astype(jnp.bfloat16)
    unpacked = projected.reshape(windows_local, WIN_TOK, heads_local, 3, HEAD_DIM)
    queries = unpacked[:, :, :, 0].transpose(0, 2, 1, 3)
    key_rows = unpacked[:, :, :, 1].transpose(0, 2, 1, 3)
    value_rows = unpacked[:, :, :, 2].transpose(0, 2, 1, 3)
    keep_scale = (
        keep_mask.reshape(windows_local, heads_local, WIN_TOK, WIN_TOK).astype(jnp.float32)
        * INV_KEEP
    )
    scores = (
        jnp.einsum("whqe,whke->whqk", queries, key_rows, preferred_element_type=jnp.float32)
        * score_scale
    )
    attn_probs = jax.nn.softmax(scores, axis=-1)
    dropped = (attn_probs * keep_scale).astype(jnp.bfloat16)
    mixed = jnp.einsum(
        "whqk,whke->whqe", dropped, value_rows, preferred_element_type=jnp.float32
    ).astype(jnp.bfloat16)
    mixed_heads = mixed.transpose(0, 2, 1, 3).reshape(tok_dev, heads_local * HEAD_DIM)
    contract = (((1,), (1,)), ((), ()))
    out_partial = lax.dot_general(
        mixed_heads, out_full, contract, preferred_element_type=jnp.float32
    )
    attended = restore(head_total(out_partial).astype(jnp.bfloat16))
    grad_heads = jnp.dot(cot_window, out_full, preferred_element_type=jnp.float32).astype(
        jnp.bfloat16
    )
    grad_rows = grad_heads.reshape(windows_local, WIN_TOK, heads_local, HEAD_DIM).transpose(
        0, 2, 1, 3
    )
    grad_probs = (
        jnp.einsum("whqe,whke->whqk", grad_rows, value_rows, preferred_element_type=jnp.float32)
        * keep_scale
    )
    inner = jnp.sum(grad_probs * attn_probs, axis=-1, keepdims=True)
    grad_scores = (score_scale * attn_probs * (grad_probs - inner)).astype(jnp.bfloat16)
    grad_query = jnp.einsum(
        "whqk,whke->whqe", grad_scores, key_rows, preferred_element_type=jnp.float32
    )
    grad_key = jnp.einsum(
        "whqk,whqe->whke", grad_scores, queries, preferred_element_type=jnp.float32
    )
    grad_value = jnp.einsum(
        "whqk,whqe->whke", dropped, grad_rows, preferred_element_type=jnp.float32
    )
    stacked = jnp.stack([grad_query, grad_key, grad_value], axis=3)
    grad_projected = (
        stacked.transpose(0, 2, 1, 3, 4)
        .reshape(tok_dev, 3 * heads_local * HEAD_DIM)
        .astype(jnp.bfloat16)
    )
    back_partial = lax.dot_general(
        grad_projected, qkv_full, contract, preferred_element_type=jnp.float32
    )
    grad_tokens = restore(head_total(back_partial).astype(jnp.bfloat16))
    over_rows = (((0,), (0,)), ((), ()))
    grad_qkv_local = lax.dot_general(
        windowed, grad_projected, over_rows, preferred_element_type=jnp.float32
    )
    grad_out_local = lax.dot_general(
        cot_window, mixed_heads, over_rows, preferred_element_type=jnp.float32
    )
    grad_qkv, grad_out = (
        lax.psum_scatter(grad_qkv_local, "seq", scatter_dimension=0, tiled=True),
        lax.psum_scatter(grad_out_local, "seq", scatter_dimension=0, tiled=True),
    )
    grad_scale = (tok_dev * seq_count) ** (-0.5)
    return (attended, grad_tokens, grad_qkv * grad_scale, grad_out * grad_scale)


def solution(mesh):
    return jax.shard_map(
        per_device,
        mesh=mesh,
        in_specs=(
            P("seq", None),
            P("seq", None),
            P("seq"),
            P("seq", "fsdp", None),
            P("seq", "fsdp"),
            P("seq", "fsdp"),
        ),
        out_specs=(P("seq", "fsdp"), P("seq", "fsdp"), P("seq", "fsdp"), P("seq", "fsdp")),
        check_vma=False,
    )
```

profile of v0, /device:TPU:2, one launch (start us, length us, event | category | flops | bytes accessed | tf_op | source)
XLA Modules:
  0.0 583.5 jit_solution(13186685068350491355)
XLA Ops:
  7.2 5.2 sort.59
  12.4 5.5 gather_fusion.4
  17.9 11.6 %all-to-all-start.2 = ((bf16[32,32,1280]{2,1,0:T(8,128)(2,1)}), bf16[32,32,1280]{2,1,0:T(8,128)(2,1)}, u32[]{:S(2)}, u32[]{:S(2)}) async-start(bf16[32,32,1280]{2,1,0:T(8,128)(2,1)} %bitcast.90), calls=%async_computation.2 | async-start | bytes 5242880 | tf_op jit(solution)/shard_map/all_to_all | solution.py:50
  29.5 8.7 %gather_fusion = bf16[1024,1280]{1,0:T(8,128)(2,1)} fusion(bf16[1024,1280]{1,0:T(8,128)(2,1)} %param.6, s32[1024]{0:T(1024)S(1)} %fusion.29), kind=kCustom, calls=%fused_computation | custom fusion | bytes 5246976 | tf_op jit(solution)/shard_map/gather | solution.py:47
  38.2 50.0 %all-to-all-done.2 = bf16[32,32,1280]{2,1,0:T(8,128)(2,1)} async-done(((bf16[32,32,1280]{2,1,0:T(8,128)(2,1)}), bf16[32,32,1280]{2,1,0:T(8,128)(2,1)}, u32[]{:S(2)}, u32[]{:S(2)}) %all-to-all-start.2) | async-done | bytes 2621472 | tf_op jit(solution)/shard_map/all_to_all | solution.py:50
  88.2 8.7 %all-to-all-start = ((bf16[32,32,1280]{2,1,0:T(8,128)(2,1)}), bf16[32,32,1280]{2,1,0:T(8,128)(2,1)}, u32[]{:S(2)}, u32[]{:S(2)}) async-start(bf16[32,32,1280]{2,1,0:T(8,128)(2,1)} %bitcast.89), calls=%async_computation | async-start | bytes 5242880 | tf_op jit(solution)/shard_map/all_to_all | solution.py:47
  103.3 4.4 sort.60
  107.6 4.4 sort.61
  112.0 87.9 %all_gather.7 = bf16[1280,160]{1,0:T(8,128)(2,1)S(1)} all-gather(bf16[40,160]{1,0:T(8,128)(2,1)S(1)} %copy-done.8), channel_id=1, replica_groups=mesh['seq'=32,'fsdp'=8] {'seq'}, dimensions={0}, use_global_device_ids=true | all-gather | bytes 422400 | tf_op jit(solution)/shard_map/all_gather | solution.py:45
  199.9 8.8 %gather_fusion.5 = bf16[1024,1280]{1,0:T(8,128)(2,1)} fusion(bf16[1024,1280]{1,0:T(8,128)(2,1)} %bitcast.12, s32[1024]{0:T(1024)S(1)} %fusion.30), kind=kCustom, calls=%fused_computation.5 | custom fusion | bytes 5246976 | tf_op jit(solution)/shard_map/gather | solution.py:50
  208.7 3.5 convolution_convert_fusion.7
  217.0 8.7 %gather_fusion.1 = bf16[1024,1280]{1,0:T(8,128)(2,1)} fusion(bf16[1024,1280]{1,0:T(8,128)(2,1)} %bitcast.1, s32[1024]{0:T(1024)S(1)} %fusion.30), kind=kCustom, calls=%fused_computation.1 | custom fusion | bytes 5246976 | tf_op jit(solution)/shard_map/gather | solution.py:47
  225.7 4.5 convolution_convert_fusion.2
  230.2 3.8 reshape.34
  253.0 4.2 copy.43
  257.2 3.9 convert_element_type.53
  261.1 4.8 convolution_convert_fusion
  265.9 4.5 copy.50
  280.9 4.5 copy.48
  286.4 3.7 fusion.52
  290.2 5.1 fusion.51
  295.4 19.4 %reduce-scatter.15.cloned.1.call-done = bf16[160,1024]{1,0:T(8,128)(2,1)} async-done(((bf16[1280,1024]{1,0:T(8,128)(2,1)}), bf16[160,1024]{1,0:T(8,128)(2,1)}) %reduce-scatter.15.cloned.1.call-update) | async-done | bytes 327696
  315.9 4.9 gather_fusion.6
  320.8 9.0 %all-to-all-start.3 = ((bf16[32,32,160]{2,1,0:T(8,128)(2,1)}), bf16[32,32,160]{2,1,0:T(8,128)(2,1)S(1)}, u32[]{:S(2)}, u32[]{:S(2)}) async-start(bf16[32,32,160]{2,1,0:T(8,128)(2,1)} %bitcast.95), calls=%async_computation.3 | async-start | bytes 1048576 | tf_op jit(solution)/shard_map/all_to_all | solution.py:40
  329.8 4.4 sort.62
  334.2 38.6 %reduce-scatter.13.cloned.1.call-done = bf16[160,1024]{1,0:T(8,128)(2,1)} async-done(((bf16[1280,1024]{1,0:T(8,128)(2,1)}), bf16[160,1024]{1,0:T(8,128)(2,1)}) %reduce-scatter.13.cloned.1.call-update) | async-done | bytes 327696
  374.7 5.7 gather_fusion.2
  380.4 9.1 %all-to-all-start.1 = ((bf16[32,32,160]{2,1,0:T(8,128)(2,1)}), bf16[32,32,160]{2,1,0:T(8,128)(2,1)}, u32[]{:S(2)}, u32[]{:S(2)}) async-start(bf16[32,32,160]{2,1,0:T(8,128)(2,1)} %bitcast.94), calls=%async_computation.1 | async-start | bytes 1048576 | tf_op jit(solution)/shard_map/all_to_all | solution.py:40
  389.6 78.1 %reduce-scatter.11.cloned.1.call-done = f32[40,160]{1,0:T(8,128)} async-done(((f32[1280,160]{1,0:T(8,128)}), f32[40,160]{1,0:T(8,128)}) %reduce-scatter.11.cloned.1.call-update) | async-done | bytes 25616 | tf_op jit(solution)/shard_map/reduce_scatter | solution.py:117
  469.1 94.0 %reduce-scatter.9.cloned.1.call-done = f32[40,480]{1,0:T(8,128)} async-done(((f32[1280,480]{1,0:T(8,128)}), f32[40,480]{1,0:T(8,128)}) %reduce-scatter.9.cloned.1.call-update) | async-done | bytes 76816 | tf_op jit(solution)/shard_map/reduce_scatter | solution.py:116
  564.6 4.9 gather_fusion.7
  571.4 4.6 gather_fusion.3
  (67 shorter events, 50.4 us)
Async XLA Ops:
  7.2 5.2 copy-start
  17.9 70.3 %all-to-all-start.2 = ((bf16[32,32,1280]{2,1,0:T(8,128)(2,1)}), bf16[32,32,1280]{2,1,0:T(8,128)(2,1)}, u32[]{:S(2)}, u32[]{:S(2)}) async-start(bf16[32,32,1280]{2,1,0:T(8,128)(2,1)} %bitcast.90), calls=%async_computation.2 | async-start | bytes 5242880 | tf_op jit(solution)/shard_map/all_to_all | solution.py:50
  88.2 128.7 %all-to-all-start = ((bf16[32,32,1280]{2,1,0:T(8,128)(2,1)}), bf16[32,32,1280]{2,1,0:T(8,128)(2,1)}, u32[]{:S(2)}, u32[]{:S(2)}) async-start(bf16[32,32,1280]{2,1,0:T(8,128)(2,1)} %bitcast.89), calls=%async_computation | async-start | bytes 5242880 | tf_op jit(solution)/shard_map/all_to_all | solution.py:47
  96.9 15.1 %copy-start.8 = (bf16[40,160]{1,0:T(8,128)(2,1)S(1)}, bf16[40,160]{1,0:T(8,128)(2,1)}, u32[]{:S(2)}) copy-start(bf16[40,160]{1,0:T(8,128)(2,1)} %param.11) | copy-start | bytes 38404
  96.9 128.7 %all-gather.2.cloned.1.call-start = ((), (), s32[]{:S(2)}) async-start(), calls=%async_computation.8 | async-start | bytes 1351680 | tf_op jit(solution)/shard_map/all_gather | solution.py:44
  97.7 217.1 %reduce-scatter.15.cloned.1.call-start = ((), (), s32[]{:S(2)}) async-start(), calls=%async_computation.12 | async-start | bytes 2949120
  246.9 2.5 copy-start.2
  246.9 2.5 copy-start.7
  249.3 1.1 copy-start.5
  249.4 1.3 copy-start.4
  249.8 1.2 copy-start.1
  249.8 1.3 copy-start.3
  270.5 102.3 %reduce-scatter.13.cloned.1.call-start = ((), (), s32[]{:S(2)}) async-start(), calls=%async_computation.11 | async-start | bytes 2949120
  285.4 1.0 copy-start.6
  285.5 182.2 %reduce-scatter.11.cloned.1.call-start = ((), (), s32[]{:S(2)}) async-start(), calls=%async_computation.10 | async-start | bytes 1351680 | tf_op jit(solution)/shard_map/reduce_scatter | solution.py:117
  290.2 272.9 %reduce-scatter.9.cloned.1.call-start = ((), (), s32[]{:S(2)}) async-start(), calls=%async_computation.9 | async-start | bytes 2703360 | tf_op jit(solution)/shard_map/reduce_scatter | solution.py:116
  320.8 59.6 %all-to-all-start.3 = ((bf16[32,32,160]{2,1,0:T(8,128)(2,1)}), bf16[32,32,160]{2,1,0:T(8,128)(2,1)S(1)}, u32[]{:S(2)}, u32[]{:S(2)}) async-start(bf16[32,32,160]{2,1,0:T(8,128)(2,1)} %bitcast.95), calls=%async_computation.3 | async-start | bytes 1048576 | tf_op jit(solution)/shard_map/all_to_all | solution.py:40
  380.4 191.0 %all-to-all-start.1 = ((bf16[32,32,160]{2,1,0:T(8,128)(2,1)}), bf16[32,32,160]{2,1,0:T(8,128)(2,1)}, u32[]{:S(2)}, u32[]{:S(2)}) async-start(bf16[32,32,160]{2,1,0:T(8,128)(2,1)} %bitcast.94), calls=%async_computation.1 | async-start | bytes 1048576 | tf_op jit(solution)/shard_map/all_to_all | solution.py:40
Sparse Core Ops, SparseCore 0:
  100.3 68.3 all-gather.1
  270.6 44.1 reduce-scatter.14
  317.3 55.4 reduce-scatter.12
  376.4 91.1 reduce-scatter.10
  471.9 91.1 reduce-scatter.8
where the time goes:
time: 585 us; the launch traced here: 583 us
  waiting for transfers between devices  281 us (48%)
  local copies, waits for them, and re-layouts  104 us (18%)
  blocking collectives  87.9 us (15%)
  starting transfers between devices  38.6 us (7%)
  matrix products  33.5 us (6%)
  other arithmetic  24.6 us (4%)
  between operations  14 us (2%)
    reduce_scatter x1, waiting for transfers between devices, per_device(): lax.psum_scatter(grad_qkv_local, 'seq', scatter_dimension=0, tiled=True)  94 us
    all_gather x1, blocking collectives, per_device(): lax.all_gather(out_weight, 'seq', axis=0, tiled=True)  87.9 us
    reduce_scatter x1, waiting for transfers between devices, per_device(): lax.psum_scatter(grad_out_local, 'seq', scatter_dimension=0, tiled=True)  78.1 us
    unnamed x7, waiting for transfers between devices  58.7 us
    all_to_all x1, waiting for transfers between devices, per_device(): lax.all_to_all(cotangent[send_order], 'seq', split_axis=0, concat_axis=0,...  50 us
    unnamed x27, local copies, waits for them, and re-layouts  23.8 us
    all_to_all x2, starting transfers between devices, restore(): lax.all_to_all(outgoing, 'seq', split_axis=0, concat_axis=0, tiled=True)  18.1 us
  transfers between devices with their start and end apart: 9, of which 5 were waited for; matrix products, arithmetic and copies ran while one was open for 17% of the time, Pallas kernels for 0%

commit v1 on v0

--- a/solution.py
+++ b/solution.py
@@ -42,7 +42,9 @@
 
     qkv_full, out_full = (
         lax.all_gather(qkv_weight, "seq", axis=0, tiled=True),
-        lax.all_gather(out_weight, "seq", axis=0, tiled=True),
+        jnp.concatenate(
+            lax.all_to_all(jnp.stack([out_weight] * lax.axis_size("seq")), "seq", 0, 0), axis=0
+        ),
     )
     windowed = lax.all_to_all(tokens[send_order], "seq", split_axis=0, concat_axis=0, tiled=True)[
         slot_recv

time: 585 us -> 566 us (0.968)
  blocking collectives: 87.9 us -> 0 us
  waiting for transfers between devices: 281 us -> 341 us
    all_gather x1 -> x0, blocking collectives: 87.9 us -> none  [per_device(): lax.all_gather(out_weight, 'seq', axis=0, tiled=True)]
    all_to_all x1, waiting for transfers between devices: 0.01 us -> 26.8 us  [per_device(): lax.all_to_all(tokens[send_order], 'seq', split_axis=0, concat_axis=0, ti...]
    all_gather x1, waiting for transfers between devices: 0.01 us -> 23 us  [per_device(): lax.all_gather(qkv_weight, 'seq', axis=0, tiled=True)]
    all_to_all x0 -> x1, starting transfers between devices: none -> 11.5 us  [per_device(): lax.all_to_all(jnp.stack([out_weight] * lax.axis_size('seq')), 'seq', 0, 0)]
    all_to_all x0 -> x1, waiting for transfers between devices: none -> 9.23 us  [per_device(): lax.all_to_all(jnp.stack([out_weight] * lax.axis_size('seq')), 'seq', 0, 0)]
    unnamed x27 -> x25, local copies, waits for them, and re-layouts: 23.8 us -> 23.8 us
  transfers between devices with their start and end apart: 9 -> 10, of which waited for: 5 -> 8; matrix products, arithmetic and copies ran while one was open for 17% -> 20% of each run, Pallas kernels for 0% -> 0%
where the time goes in v1:
time: 566 us; the launch traced here: 564 us
  waiting for transfers between devices  341 us (60%)
  local copies, waits for them, and re-layouts  107 us (19%)
  starting transfers between devices  43 us (8%)
  matrix products  33.5 us (6%)
  other arithmetic  25.3 us (4%)
  between operations  14 us (2%)
    reduce_scatter x1, waiting for transfers between devices, per_device(): lax.psum_scatter(grad_qkv_local, 'seq', scatter_dimension=0, tiled=True)  93.8 us
    reduce_scatter x1, waiting for transfers between devices, per_device(): lax.psum_scatter(grad_out_local, 'seq', scatter_dimension=0, tiled=True)  77.9 us
    unnamed x7, waiting for transfers between devices  57.3 us
    all_to_all x1, waiting for transfers between devices, per_device(): lax.all_to_all(cotangent[send_order], 'seq', split_axis=0, concat_axis=0,...  53.5 us
    all_to_all x1, waiting for transfers between devices, per_device(): lax.all_to_all(tokens[send_order], 'seq', split_axis=0, concat_axis=0, ti...  26.8 us
    unnamed x25, local copies, waits for them, and re-layouts  23.8 us
    all_gather x1, waiting for transfers between devices, per_device(): lax.all_gather(qkv_weight, 'seq', axis=0, tiled=True)  23 us
    all_to_all x2, starting transfers between devices, restore(): lax.all_to_all(outgoing, 'seq', split_axis=0, concat_axis=0, tiled=True)  18.2 us
  transfers between devices with their start and end apart: 10, of which 8 were waited for; matrix products, arithmetic and copies ran while one was open for 20% of the time, Pallas kernels for 0%

profile of v1, /device:TPU:2, one launch (start us, length us, event | category | flops | bytes accessed | tf_op | source)
XLA Modules:
  0.0 564.2 jit_solution(10413388286708288582)
XLA Ops:
  8.9 11.5 %all-to-all-start.1 = ((bf16[32,40,160]{2,1,0:T(8,128)(2,1)}), bf16[32,40,160]{2,1,0:T(8,128)(2,1)S(1)}, u32[]{:S(2)}, u32[]{:S(2)}) async-start(bf16[32,40,160]{2,1,0:T(8,128)(2,1)} %stack.14), calls=%async_computation.1 | async-start | bytes 1310720 | tf_op jit(solution)/shard_map/all_to_all | solution.py:46
  20.5 5.1 sort.59
  25.5 5.5 gather_fusion.4
  31.0 9.2 %all-to-all-done.1 = bf16[32,40,160]{2,1,0:T(8,128)(2,1)S(1)} async-done(((bf16[32,40,160]{2,1,0:T(8,128)(2,1)}), bf16[32,40,160]{2,1,0:T(8,128)(2,1)S(1)}, u32[]{:S(2)}, u32[]{:S(2)}) %all-to-all-start.1) | async-done | bytes 409632 | tf_op jit(solution)/shard_map/all_to_all | solution.py:46
  40.2 6.1 %all-to-all-start.3 = ((bf16[32,32,1280]{2,1,0:T(8,128)(2,1)}), bf16[32,32,1280]{2,1,0:T(8,128)(2,1)}, u32[]{:S(2)}, u32[]{:S(2)}) async-start(bf16[32,32,1280]{2,1,0:T(8,128)(2,1)} %bitcast.91), calls=%async_computation.3 | async-start | bytes 5242880 | tf_op jit(solution)/shard_map/all_to_all | solution.py:52
  46.3 8.7 %gather_fusion = bf16[1024,1280]{1,0:T(8,128)(2,1)} fusion(bf16[1024,1280]{1,0:T(8,128)(2,1)} %param.6, s32[1024]{0:T(1024)S(1)} %fusion.29), kind=kCustom, calls=%fused_computation | custom fusion | bytes 5246976 | tf_op jit(solution)/shard_map/gather | solution.py:49
  55.0 53.5 %all-to-all-done.3 = bf16[32,32,1280]{2,1,0:T(8,128)(2,1)} async-done(((bf16[32,32,1280]{2,1,0:T(8,128)(2,1)}), bf16[32,32,1280]{2,1,0:T(8,128)(2,1)}, u32[]{:S(2)}, u32[]{:S(2)}) %all-to-all-start.3) | async-done | bytes 2621472 | tf_op jit(solution)/shard_map/all_to_all | solution.py:52
  108.5 7.1 %all-to-all-start = ((bf16[32,32,1280]{2,1,0:T(8,128)(2,1)}), bf16[32,32,1280]{2,1,0:T(8,128)(2,1)}, u32[]{:S(2)}, u32[]{:S(2)}) async-start(bf16[32,32,1280]{2,1,0:T(8,128)(2,1)} %bitcast.90), calls=%async_computation | async-start | bytes 5242880 | tf_op jit(solution)/shard_map/all_to_all | solution.py:49
  123.7 4.4 sort.60
  128.1 4.4 sort.61
  132.5 8.9 %gather_fusion.5 = bf16[1024,1280]{1,0:T(8,128)(2,1)} fusion(bf16[1024,1280]{1,0:T(8,128)(2,1)} %bitcast.13, s32[1024]{0:T(1024)S(1)} %fusion.30), kind=kCustom, calls=%fused_computation.5 | custom fusion | bytes 5246976 | tf_op jit(solution)/shard_map/gather | solution.py:52
  149.6 26.8 %all-to-all-done = bf16[32,32,1280]{2,1,0:T(8,128)(2,1)} async-done(((bf16[32,32,1280]{2,1,0:T(8,128)(2,1)}), bf16[32,32,1280]{2,1,0:T(8,128)(2,1)}, u32[]{:S(2)}, u32[]{:S(2)}) %all-to-all-start) | async-done | bytes 2621472 | tf_op jit(solution)/shard_map/all_to_all | solution.py:49
  176.3 8.7 %gather_fusion.1 = bf16[1024,1280]{1,0:T(8,128)(2,1)} fusion(bf16[1024,1280]{1,0:T(8,128)(2,1)} %bitcast.1, s32[1024]{0:T(1024)S(1)} %fusion.30), kind=kCustom, calls=%fused_computation.1 | custom fusion | bytes 5246976 | tf_op jit(solution)/shard_map/gather | solution.py:49
  185.0 23.0 %all-gather.2.cloned.1.call-done = bf16[1280,480]{1,0:T(8,128)(2,1)} async-done(((bf16[40,480]{1,0:T(8,128)(2,1)}), bf16[1280,480]{1,0:T(8,128)(2,1)}) %all-gather.2.cloned.1.call-update) | async-done | bytes 1228816 | tf_op jit(solution)/shard_map/all_gather | solution.py:44
  208.0 4.5 convolution_convert_fusion.2
  235.4 4.2 copy.43
  239.5 3.9 convert_element_type.53
  243.4 4.8 convolution_convert_fusion
  248.3 4.5 copy.50
  263.3 4.5 copy.48
  272.5 5.1 fusion.51
  277.6 17.7 %reduce-scatter.15.cloned.1.call-done = bf16[160,1024]{1,0:T(8,128)(2,1)} async-done(((bf16[1280,1024]{1,0:T(8,128)(2,1)}), bf16[160,1024]{1,0:T(8,128)(2,1)}) %reduce-scatter.15.cloned.1.call-update) | async-done | bytes 327696
  296.5 4.9 gather_fusion.6
  301.4 9.0 %all-to-all-start.4 = ((bf16[32,32,160]{2,1,0:T(8,128)(2,1)}), bf16[32,32,160]{2,1,0:T(8,128)(2,1)S(1)}, u32[]{:S(2)}, u32[]{:S(2)}) async-start(bf16[32,32,160]{2,1,0:T(8,128)(2,1)} %bitcast.98), calls=%async_computation.4 | async-start | bytes 1048576 | tf_op jit(solution)/shard_map/all_to_all | solution.py:40
  310.4 4.4 sort.62
  314.8 38.9 %reduce-scatter.13.cloned.1.call-done = bf16[160,1024]{1,0:T(8,128)(2,1)} async-done(((bf16[1280,1024]{1,0:T(8,128)(2,1)}), bf16[160,1024]{1,0:T(8,128)(2,1)}) %reduce-scatter.13.cloned.1.call-update) | async-done | bytes 327696
  355.7 5.7 %gather_fusion.2 = bf16[1024,160]{1,0:T(8,128)(2,1)} fusion(bf16[1024,160]{1,0:T(8,128)(2,1)} %copy.49, s32[1024]{0:T(1024)S(1)} %fusion.31), kind=kCustom, calls=%fused_computation.2 | custom fusion | bytes 659456 | tf_op jit(solution)/shard_map/gather | solution.py:39
  361.3 9.2 %all-to-all-start.2 = ((bf16[32,32,160]{2,1,0:T(8,128)(2,1)}), bf16[32,32,160]{2,1,0:T(8,128)(2,1)}, u32[]{:S(2)}, u32[]{:S(2)}) async-start(bf16[32,32,160]{2,1,0:T(8,128)(2,1)} %bitcast.97), calls=%async_computation.2 | async-start | bytes 1048576 | tf_op jit(solution)/shard_map/all_to_all | solution.py:40
  370.6 77.9 %reduce-scatter.11.cloned.1.call-done = f32[40,160]{1,0:T(8,128)} async-done(((f32[1280,160]{1,0:T(8,128)}), f32[40,160]{1,0:T(8,128)}) %reduce-scatter.11.cloned.1.call-update) | async-done | bytes 25616 | tf_op jit(solution)/shard_map/reduce_scatter | solution.py:119
  449.9 93.8 %reduce-scatter.9.cloned.1.call-done = f32[40,480]{1,0:T(8,128)} async-done(((f32[1280,480]{1,0:T(8,128)}), f32[40,480]{1,0:T(8,128)}) %reduce-scatter.9.cloned.1.call-update) | async-done | bytes 76816 | tf_op jit(solution)/shard_map/reduce_scatter | solution.py:118
  545.3 4.9 gather_fusion.7
  552.2 4.6 gather_fusion.3
  (67 shorter events, 65.1 us)
Async XLA Ops:
  7.2 18.3 %copy-start = (bf16[1024,1280]{1,0:T(8,128)(2,1)S(1)}, bf16[1024,1280]{1,0:T(8,128)(2,1)}, u32[]{:S(2)}) copy-start(bf16[1024,1280]{1,0:T(8,128)(2,1)} %param.7) | copy-start | bytes 7864324
  8.9 31.3 %all-to-all-start.1 = ((bf16[32,40,160]{2,1,0:T(8,128)(2,1)}), bf16[32,40,160]{2,1,0:T(8,128)(2,1)S(1)}, u32[]{:S(2)}, u32[]{:S(2)}) async-start(bf16[32,40,160]{2,1,0:T(8,128)(2,1)} %stack.14), calls=%async_computation.1 | async-start | bytes 1310720 | tf_op jit(solution)/shard_map/all_to_all | solution.py:46
  40.2 68.3 %all-to-all-start.3 = ((bf16[32,32,1280]{2,1,0:T(8,128)(2,1)}), bf16[32,32,1280]{2,1,0:T(8,128)(2,1)}, u32[]{:S(2)}, u32[]{:S(2)}) async-start(bf16[32,32,1280]{2,1,0:T(8,128)(2,1)} %bitcast.91), calls=%async_computation.3 | async-start | bytes 5242880 | tf_op jit(solution)/shard_map/all_to_all | solution.py:52
  108.5 67.9 %all-to-all-start = ((bf16[32,32,1280]{2,1,0:T(8,128)(2,1)}), bf16[32,32,1280]{2,1,0:T(8,128)(2,1)}, u32[]{:S(2)}, u32[]{:S(2)}) async-start(bf16[32,32,1280]{2,1,0:T(8,128)(2,1)} %bitcast.90), calls=%async_computation | async-start | bytes 5242880 | tf_op jit(solution)/shard_map/all_to_all | solution.py:49
  115.6 92.4 %all-gather.2.cloned.1.call-start = ((), (), s32[]{:S(2)}) async-start(), calls=%async_computation.9 | async-start | bytes 1351680 | tf_op jit(solution)/shard_map/all_gather | solution.py:44
  116.3 179.0 %reduce-scatter.15.cloned.1.call-start = ((), (), s32[]{:S(2)}) async-start(), calls=%async_computation.13 | async-start | bytes 2949120
  229.2 2.5 copy-start.2
  229.2 2.5 copy-start.7
  231.7 1.1 copy-start.5
  231.7 1.3 copy-start.4
  232.1 1.2 copy-start.1
  232.2 1.3 copy-start.3
  252.8 100.9 %reduce-scatter.13.cloned.1.call-start = ((), (), s32[]{:S(2)}) async-start(), calls=%async_computation.12 | async-start | bytes 2949120
  267.8 1.0 copy-start.6
  267.8 180.7 %reduce-scatter.11.cloned.1.call-start = ((), (), s32[]{:S(2)}) async-start(), calls=%async_computation.11 | async-start | bytes 1351680 | tf_op jit(solution)/shard_map/reduce_scatter | solution.py:119
  272.5 271.3 %reduce-scatter.9.cloned.1.call-start = ((), (), s32[]{:S(2)}) async-start(), calls=%async_computation.10 | async-start | bytes 2703360 | tf_op jit(solution)/shard_map/reduce_scatter | solution.py:118
  301.4 59.9 %all-to-all-start.4 = ((bf16[32,32,160]{2,1,0:T(8,128)(2,1)}), bf16[32,32,160]{2,1,0:T(8,128)(2,1)S(1)}, u32[]{:S(2)}, u32[]{:S(2)}) async-start(bf16[32,32,160]{2,1,0:T(8,128)(2,1)} %bitcast.98), calls=%async_computation.4 | async-start | bytes 1048576 | tf_op jit(solution)/shard_map/all_to_all | solution.py:40
  361.3 190.8 %all-to-all-start.2 = ((bf16[32,32,160]{2,1,0:T(8,128)(2,1)}), bf16[32,32,160]{2,1,0:T(8,128)(2,1)}, u32[]{:S(2)}, u32[]{:S(2)}) async-start(bf16[32,32,160]{2,1,0:T(8,128)(2,1)} %bitcast.97), calls=%async_computation.2 | async-start | bytes 1048576 | tf_op jit(solution)/shard_map/all_to_all | solution.py:40
Sparse Core Ops, SparseCore 0:
  118.9 89.0 all-gather.1
  252.9 42.3 reduce-scatter.14
  297.9 55.7 reduce-scatter.12
  357.3 91.1 reduce-scatter.10
  452.7 90.9 reduce-scatter.8
